TPU v7x, 512 devices: a whole 4x8x8 slice. The times are simulated.
512 devices in a mesh: row: 32 (over z_lo, x, core), col: 16 (over z_hi, y).
Axes of the slice: x: 4, y: 8, z: 8 (z_hi: 2, z_lo: 4; z = z_hi * 4 + z_lo), core: 2. Of those that a mesh axis runs over, the one named last changes fastest.
Arguments:
- state: float32 [32, 2, 16, 256, 256], P('row', None, 'col'), may hold values from -6 to 6
- a_tiles: float32 [32, 2, 16, 256, 256], P('row', None, 'col'), may hold values from -0.375 to 0.375
- inverses: float32 [32, 256, 256], P('row'), may hold values from -0.225 to 1.025
Outputs:
- state_out: float32 [32, 2, 16, 256, 256], P('row', None, 'col')
All inputs are finite; a program needn't handle non-finite values.
Results may differ from a plain program's by a relative error of at most 0.0001.
Values sent between devices are 32-bit elements; how exact they have to be, the bound alone decides.
A program may use at most 64 MiB of HBM per device.

v0:
```python
import jax
import jax.numpy as jnp
from jax import lax
from jax.sharding import PartitionSpec as P

FRONTS = 3
DOUBLINGS = 5
HIGH = lax.Precision.HIGHEST
shift_half = 0.5


def swapped(value, axis, stride):
    mask = 2**stride
    pairs = [(source, source ^ mask) for source in range(lax.axis_size(axis))]
    return lax.ppermute(value, axis, pairs)


def passed_along(block, axis, distance):
    devices = range(lax.axis_size(axis))
    route = [((i - distance) % len(devices), i) for i in devices]
    return lax.ppermute(block, axis, route)


def spread(value, axis, source):
    kept = jnp.where(lax.axis_index(axis) == source, value, 0).astype(value.dtype)
    return lax.psum(kept, axis)


def product(left, right):
    return jnp.dot(left, right, precision=HIGH, preferred_element_type=jnp.float32)


def product_transposed(left, right):
    return lax.dot_general(
        left, right, (((1,), (1,)), ((), ())), precision=HIGH, preferred_element_type=jnp.float32
    )


def batched_product(left, right):
    return jnp.einsum(
        "nab,nbc->nac", left, right, precision=HIGH, preferred_element_type=jnp.float32
    )


def across_cols(pieces):
    return lax.all_to_all(pieces, "col", split_axis=1, concat_axis=1, tiled=True)


def mirrored(tile_set):
    slot_count = tile_set.shape[0]
    tile_order = tile_set.shape[1]
    col_count = lax.axis_size("col")
    slab_rows = tile_order // col_count
    section_one = across_cols(tile_set.reshape(slot_count, col_count, slab_rows, tile_order))
    by_target = section_one.reshape(slot_count * col_count, slab_rows, tile_order)
    section_two = lax.all_to_all(by_target, "row", split_axis=0, concat_axis=0, tiled=True)
    section_three = across_cols(section_two.reshape(slot_count, col_count, slab_rows, tile_order))
    return section_three.reshape(slot_count, tile_order, tile_order)


def flipped(tile_set, col_count):
    levels = col_count.bit_length() - 1
    for bit_pos in range(levels):
        tile_set = swapped(tile_set, "col", bit_pos)
    return tile_set


def per_device(state, a_tiles, inverses):
    slot_count = state.shape[1]
    tile_order = state.shape[3]
    col_count = lax.axis_size("col")
    height = lax.axis_size("row")
    row_here = lax.axis_index("row")
    col_here = lax.axis_index("col")
    current = state.reshape(slot_count, tile_order, tile_order)
    coupling = a_tiles.reshape(slot_count, tile_order, tile_order)
    own_inverse = inverses.reshape(tile_order, tile_order)
    identity_tile = jnp.eye(tile_order, dtype=jnp.float32)
    left_powers = [identity_tile - shift_half * own_inverse]
    for level in range(DOUBLINGS - 1):
        left_powers.append(product(left_powers[-1], left_powers[-1]))
    column_inverse = mirrored(jnp.broadcast_to(own_inverse, (slot_count, tile_order, tile_order)))
    right_list = [identity_tile[None] - shift_half * column_inverse]
    for level in range(DOUBLINGS - 1):
        right_list.append(batched_product(right_list[-1], right_list[-1]))
    right_powers = jnp.stack(right_list)
    tile_cols = jnp.arange(slot_count, dtype=jnp.int32) * col_count + col_here
    tile_sum = row_here + tile_cols
    for front_step in range(FRONTS):
        front_sum = height - 1 - front_step
        source_a = flipped(coupling, col_count)
        if front_step > 0:
            source_a = passed_along(source_a, "col", -front_step)
        front_col = front_sum - row_here
        front_slot = jnp.clip(front_col // col_count, 0, slot_count - 1)
        own_tile = lax.dynamic_index_in_dim(current, front_slot, 0, keepdims=False)
        mirror = mirrored(current)
        far_tile = lax.dynamic_index_in_dim(mirror, front_slot, 0, keepdims=False)
        right_side = own_tile + far_tile.T
        right_inverse = lax.dynamic_index_in_dim(column_inverse, front_slot, 0, keepdims=False)
        powers_here = lax.dynamic_index_in_dim(right_powers, front_slot, 1, keepdims=False)
        solution = shift_half * product_transposed(product(own_inverse, right_side), right_inverse)
        for level in range(DOUBLINGS):
            solution = solution + product_transposed(
                product(left_powers[level], solution), powers_here[level]
            )
        passed = []
        for slot_pos in range(slot_count):
            root_row = jnp.clip(front_sum - tile_cols[slot_pos], 0, height - 1)
            passed.append(spread(solution, "row", root_row))
        below_rows = front_sum - tile_cols
        a_slot = jnp.clip(below_rows // col_count, 0, slot_count - 1)
        a_pick = jnp.take(source_a, a_slot, axis=0)
        update = batched_product(a_pick, jnp.stack(passed))
        shrink = (tile_sum < front_sum)[:, None, None]
        place = (tile_sum == front_sum)[:, None, None]
        current = jnp.where(shrink, current - update, jnp.where(place, solution[None], current))
    return current.reshape(state.shape)


def solution(mesh):
    in_specs = (
        P("row", None, "col", None, None),
        P("row", None, "col", None, None),
        P("row", None, None),
    )
    out_specs = P("row", None, "col", None, None)
    return jax.shard_map(
        per_device, mesh=mesh, in_specs=in_specs, out_specs=out_specs, check_vma=False
    )
```

profile of v0, /device:TPU:1, one launch (start us, length us, event | category | flops | bytes accessed | tf_op | source)
XLA Modules:
  0.0 1221.0 jit_solution(3985047102242037960)
XLA Ops:
  7.6 34.1 %all_to_all.60 = f32[2,16,16,256]{3,2,0,1:T(8,128)S(1)} all-to-all(f32[2,16,16,256]{3,2,0,1:T(8,128)S(1)} %copy.25), channel_id=1, replica_groups=mesh['row'=32,'col'=16] {'col'}, dimensions={1} | all-to-all | bytes 1048576 | tf_op jit(solution)/shard_map/all_to_all | solution.py:46
  50.0 16.1 %all-to-all-done.3 = f32[2,16,16,256]{3,2,0,1:T(8,128)S(1)} async-done(((f32[2,16,16,256]{3,2,0,1:T(8,128)}), f32[2,16,16,256]{3,2,0,1:T(8,128)S(1)}, u32[]{:S(2)}, u32[]{:S(2)}) %all-to-all-start.3) | async-done | bytes 524320 | tf_op jit(solution)/shard_map/all_to_all | solution.py:46
  66.1 10.6 all-to-all-start.1
  77.6 15.6 %all-to-all-done.1 = f32[32,16,256]{2,1,0:T(8,128)S(1)} async-done(((f32[32,16,256]{2,1,0:T(8,128)}), f32[32,16,256]{2,1,0:T(8,128)S(1)}, u32[]{:S(2)}, u32[]{:S(2)}) %all-to-all-start.1) | async-done | bytes 524320 | tf_op jit(solution)/shard_map/all_to_all | solution.py:56
  101.4 12.4 %all-to-all-done.4 = f32[32,16,256]{2,1,0:T(8,128)S(1)} async-done(((f32[32,16,256]{2,1,0:T(8,128)}), f32[32,16,256]{2,1,0:T(8,128)S(1)}, u32[]{:S(2)}, u32[]{:S(2)}) %all-to-all-start.4) | async-done | bytes 524320 | tf_op jit(solution)/shard_map/all_to_all | solution.py:56
  124.1 13.2 %all-to-all-done.2 = f32[2,16,16,256]{3,2,0,1:T(8,128)S(1)} async-done(((f32[2,16,16,256]{3,2,0,1:T(8,128)}), f32[2,16,16,256]{3,2,0,1:T(8,128)S(1)}, u32[]{:S(2)}, u32[]{:S(2)}) %all-to-all-start.2) | async-done | bytes 524320 | tf_op jit(solution)/shard_map/all_to_all | solution.py:46
  137.4 5.7 all-to-all-start.5
  143.8 15.3 %collective-permute-done.1 = f32[2,256,256]{2,1,0:T(8,128)} collective-permute-done((f32[2,256,256]{2,1,0:T(8,128)}, f32[2,256,256]{2,1,0:T(8,128)}, u32[]{:S(2)}, u32[]{:S(2)}) %collective-permute-start.1) | collective-permute-done | bytes 524320 | tf_op jit(solution)/shard_map/ppermute | solution.py:15
  159.0 8.0 collective-permute-start.2
  169.1 20.2 %collective-permute-done.2 = f32[2,256,256]{2,1,0:T(8,128)} collective-permute-done((f32[2,256,256]{2,1,0:T(8,128)}, f32[2,256,256]{2,1,0:T(8,128)}, u32[]{:S(2)}, u32[]{:S(2)}) %collective-permute-start.2) | collective-permute-done | bytes 524320 | tf_op jit(solution)/shard_map/ppermute | solution.py:15
  200.8 11.9 collective-permute-done.3
  215.1 269.7 %all-reduce.11.cloned.1.call-done = (f32[1,256,256]{2,1,0:T(8,128)}, f32[1,256,256]{2,1,0:T(8,128)}) async-done(((f32[1,256,256]{2,1,0:T(8,128)}, f32[1,256,256]{2,1,0:T(8,128)}), (f32[1,256,256]{2,1,0:T(8,128)}, f32[1,256,256]{2,1,0:T(8,128)})) %all-reduce.11.cloned.1.call-update) | async-done | bytes 524304 | tf_op jit(solution)/shard_map/psum | solution.py:26
  486.7 26.0 %all_to_all.61 = f32[2,16,16,256]{3,2,0,1:T(8,128)S(1)} all-to-all(f32[2,16,16,256]{3,2,0,1:T(8,128)S(1)} %copy.34), channel_id=1, replica_groups=mesh['row'=32,'col'=16] {'col'}, dimensions={1} | all-to-all | bytes 1048576 | tf_op jit(solution)/shard_map/all_to_all | solution.py:46
  512.8 23.9 %all_to_all.62 = f32[32,16,256]{2,1,0:T(8,128)S(1)} all-to-all(f32[32,16,256]{2,1,0:T(8,128)S(1)} %bitcast.223), channel_id=1, replica_groups=mesh['row'=32,'col'=16] {'row'}, dimensions={0} | all-to-all | bytes 1048576 | tf_op jit(solution)/shard_map/all_to_all | solution.py:56
  543.8 9.5 collective-permute-start.4
  553.3 8.2 all-to-all-done.8
  568.1 9.1 collective-permute-done.4
  579.5 270.4 %all-reduce.9.cloned.1.call-done = (f32[1,256,256]{2,1,0:T(8,128)}, f32[1,256,256]{2,1,0:T(8,128)}) async-done(((f32[1,256,256]{2,1,0:T(8,128)}, f32[1,256,256]{2,1,0:T(8,128)}), (f32[1,256,256]{2,1,0:T(8,128)}, f32[1,256,256]{2,1,0:T(8,128)})) %all-reduce.9.cloned.1.call-update) | async-done | bytes 524304 | tf_op jit(solution)/shard_map/psum | solution.py:26
  851.9 26.0 %all_to_all.63 = f32[2,16,16,256]{3,2,0,1:T(8,128)S(1)} all-to-all(f32[2,16,16,256]{3,2,0,1:T(8,128)S(1)} %copy.39), channel_id=1, replica_groups=mesh['row'=32,'col'=16] {'col'}, dimensions={1} | all-to-all | bytes 1048576 | tf_op jit(solution)/shard_map/all_to_all | solution.py:46
  878.0 23.9 %all_to_all.64 = f32[32,16,256]{2,1,0:T(8,128)S(1)} all-to-all(f32[32,16,256]{2,1,0:T(8,128)S(1)} %bitcast.225), channel_id=1, replica_groups=mesh['row'=32,'col'=16] {'row'}, dimensions={0} | all-to-all | bytes 1048576 | tf_op jit(solution)/shard_map/all_to_all | solution.py:56
  909.0 10.5 collective-permute-start.5
  919.4 7.3 all-to-all-done.11
  933.3 11.4 collective-permute-done.5
  945.3 266.6 %all-reduce.7.cloned.1.call-done = (f32[1,256,256]{2,1,0:T(8,128)}, f32[1,256,256]{2,1,0:T(8,128)}) async-done(((f32[1,256,256]{2,1,0:T(8,128)}, f32[1,256,256]{2,1,0:T(8,128)}), (f32[1,256,256]{2,1,0:T(8,128)}, f32[1,256,256]{2,1,0:T(8,128)})) %all-reduce.7.cloned.1.call-update) | async-done | bytes 524304 | tf_op jit(solution)/shard_map/psum | solution.py:26
  (120 shorter events, 77.5 us)
Async XLA Ops:
  43.5 53.8 %copy-start.5 = (f32[1,2,1,256,256]{4,3,2,1,0:T(8,128)S(1)}, f32[1,2,1,256,256]{4,3,2,1,0:T(8,128)}, u32[]{:S(2)}) copy-start(f32[1,2,1,256,256]{4,3,2,1,0:T(8,128)} %param.6) | copy-start | bytes 1572868
  43.5 22.6 %all-to-all-start.3 = ((f32[2,16,16,256]{3,2,0,1:T(8,128)}), f32[2,16,16,256]{3,2,0,1:T(8,128)S(1)}, u32[]{:S(2)}, u32[]{:S(2)}) async-start(f32[2,16,16,256]{3,2,0,1:T(8,128)} %broadcast_in_dim.91), calls=%async_computation.3 | async-start | bytes 1048576 | tf_op jit(solution)/shard_map/all_to_all | solution.py:46
  66.1 52.2 %copy-start = (f32[1,256,256]{2,1,0:T(8,128)S(1)}, f32[1,256,256]{2,1,0:T(8,128)}, u32[]{:S(2)}) copy-start(f32[1,256,256]{2,1,0:T(8,128)} %param.7) | copy-start | bytes 786436
  66.1 27.1 %all-to-all-start.1 = ((f32[32,16,256]{2,1,0:T(8,128)}), f32[32,16,256]{2,1,0:T(8,128)S(1)}, u32[]{:S(2)}, u32[]{:S(2)}) async-start(f32[32,16,256]{2,1,0:T(8,128)} %bitcast.5), calls=%async_computation.1 | async-start | bytes 1048576 | tf_op jit(solution)/shard_map/all_to_all | solution.py:56
  93.2 20.6 %all-to-all-start.4 = ((f32[32,16,256]{2,1,0:T(8,128)}), f32[32,16,256]{2,1,0:T(8,128)S(1)}, u32[]{:S(2)}, u32[]{:S(2)}) async-start(f32[32,16,256]{2,1,0:T(8,128)} %bitcast.12), calls=%async_computation.4 | async-start | bytes 1048576 | tf_op jit(solution)/shard_map/all_to_all | solution.py:56
  97.3 21.4 %collective-permute-start = (f32[2,256,256]{2,1,0:T(8,128)S(1)}, f32[2,256,256]{2,1,0:T(8,128)}, u32[]{:S(2)}, u32[]{:S(2)}) collective-permute-start(f32[2,256,256]{2,1,0:T(8,128)S(1)} %bitcast.230), channel_id=1, source_target_pairs={{0,1},{1,0},{2,3},{3,2},{4,5},{5,4},{6,7},{7,6},{8,9},{9,8},{10,11... | collective-permute-start | bytes 1572872 | tf_op jit(solution)/shard_map/ppermute | solution.py:15
  113.7 23.6 %all-to-all-start.2 = ((f32[2,16,16,256]{3,2,0,1:T(8,128)}), f32[2,16,16,256]{3,2,0,1:T(8,128)S(1)}, u32[]{:S(2)}, u32[]{:S(2)}) async-start(f32[2,16,16,256]{3,2,0,1:T(8,128)} %copy.27), calls=%async_computation.2 | async-start | bytes 1048576 | tf_op jit(solution)/shard_map/all_to_all | solution.py:46
  118.7 40.3 %collective-permute-start.1 = (f32[2,256,256]{2,1,0:T(8,128)}, f32[2,256,256]{2,1,0:T(8,128)}, u32[]{:S(2)}, u32[]{:S(2)}) collective-permute-start(f32[2,256,256]{2,1,0:T(8,128)} %collective-permute-done), channel_id=1, source_target_pairs={{0,2},{1,3},{2,0},{3,1},{4,6},{5,7},{6,4},{7,5},{8,10},{9,11},{10,... | collective-permute-start | bytes 1572872 | tf_op jit(solution)/shard_map/ppermute | solution.py:15
  124.1 67.4 %copy-start.4 = (f32[1,2,1,256,256]{4,3,2,1,0:T(8,128)S(1)}, f32[1,2,1,256,256]{4,3,2,1,0:T(8,128)}, u32[]{:S(2)}) copy-start(f32[1,2,1,256,256]{4,3,2,1,0:T(8,128)} %param.5) | copy-start | bytes 1572868
  137.4 54.8 %all-to-all-start.5 = ((f32[2,16,16,256]{3,2,0,1:T(8,128)}), f32[2,16,16,256]{3,2,0,1:T(8,128)S(1)}, u32[]{:S(2)}, u32[]{:S(2)}) async-start(f32[2,16,16,256]{3,2,0,1:T(8,128)} %copy.31), calls=%async_computation.5 | async-start | bytes 1048576 | tf_op jit(solution)/shard_map/all_to_all | solution.py:46
  143.1 341.7 %all-reduce.11.cloned.1.call-start = ((), (), s32[]{:S(2)}) async-start(), calls=%async_computation.14 | async-start | bytes 1048576 | tf_op jit(solution)/shard_map/psum | solution.py:26
  159.0 30.2 %collective-permute-start.2 = (f32[2,256,256]{2,1,0:T(8,128)}, f32[2,256,256]{2,1,0:T(8,128)}, u32[]{:S(2)}, u32[]{:S(2)}) collective-permute-start(f32[2,256,256]{2,1,0:T(8,128)} %collective-permute-done.1), channel_id=1, source_target_pairs={{0,4},{1,5},{2,6},{3,7},{4,0},{5,1},{6,2},{7,3},{8,12},{9,13},{10,... | collective-permute-start | bytes 1572872 | tf_op jit(solution)/shard_map/ppermute | solution.py:15
  189.3 23.4 %collective-permute-start.3 = (f32[2,256,256]{2,1,0:T(8,128)}, f32[2,256,256]{2,1,0:T(8,128)}, u32[]{:S(2)}, u32[]{:S(2)}) collective-permute-start(f32[2,256,256]{2,1,0:T(8,128)} %collective-permute-done.2), channel_id=1, source_target_pairs={{0,8},{1,9},{2,10},{3,11},{4,12},{5,13},{6,14},{7,15},{8,0},{9,1},... | collective-permute-start | bytes 1572872 | tf_op jit(solution)/shard_map/ppermute | solution.py:15
  196.1 3.3 copy-start.1
  537.5 24.0 %all-to-all-start.8 = ((f32[2,16,16,256]{3,2,0,1:T(8,128)}), f32[2,16,16,256]{3,2,0,1:T(8,128)S(1)}, u32[]{:S(2)}, u32[]{:S(2)}) async-start(f32[2,16,16,256]{3,2,0,1:T(8,128)} %copy.36), calls=%async_computation.8 | async-start | bytes 1048576 | tf_op jit(solution)/shard_map/all_to_all | solution.py:46
  542.4 307.6 %all-reduce.9.cloned.1.call-start = ((), (), s32[]{:S(2)}) async-start(), calls=%async_computation.13 | async-start | bytes 1048576 | tf_op jit(solution)/shard_map/psum | solution.py:26
  543.8 33.4 %collective-permute-start.4 = (f32[2,256,256]{2,1,0:T(8,128)}, f32[2,256,256]{2,1,0:T(8,128)}, u32[]{:S(2)}, u32[]{:S(2)}) collective-permute-start(f32[2,256,256]{2,1,0:T(8,128)} %collective-permute-done.3), channel_id=1, source_target_pairs={{1,0},{2,1},{3,2},{4,3},{5,4},{6,5},{7,6},{8,7},{9,8},{10,9},{11,1... | collective-permute-start | bytes 1572872 | tf_op jit(solution)/shard_map/ppermute | solution.py:21
  561.7 1.7 copy-start.2
  902.8 24.0 %all-to-all-start.11 = ((f32[2,16,16,256]{3,2,0,1:T(8,128)}), f32[2,16,16,256]{3,2,0,1:T(8,128)S(1)}, u32[]{:S(2)}, u32[]{:S(2)}) async-start(f32[2,16,16,256]{3,2,0,1:T(8,128)} %copy.41), calls=%async_computation.11 | async-start | bytes 1048576 | tf_op jit(solution)/shard_map/all_to_all | solution.py:46
  907.6 304.3 %all-reduce.7.cloned.1.call-start = ((), (), s32[]{:S(2)}) async-start(), calls=%async_computation.12 | async-start | bytes 1048576 | tf_op jit(solution)/shard_map/psum | solution.py:26
  909.0 35.8 %collective-permute-start.5 = (f32[2,256,256]{2,1,0:T(8,128)}, f32[2,256,256]{2,1,0:T(8,128)S(1)}, u32[]{:S(2)}, u32[]{:S(2)}) collective-permute-start(f32[2,256,256]{2,1,0:T(8,128)} %collective-permute-done.3), channel_id=1, source_target_pairs={{2,0},{3,1},{4,2},{5,3},{6,4},{7,5},{8,6},{9,7},{10,8},{11,9},{12,... | collective-permute-start | bytes 1572872 | tf_op jit(solution)/shard_map/ppermute | solution.py:21
  926.9 1.7 copy-start.3
Sparse Core Ops, SparseCore 0:
  200.8 283.9 all-reduce.10
  568.1 281.8 all-reduce.8
  933.3 278.5 all-reduce.6
where the time goes:
time: 1220 us
  waiting for transfers between devices  948 us (78%)
  blocking collectives  134 us (11%)
  starting transfers between devices  77.8 us (6%)
  matrix products  26.2 us (2%)
  between operations  17.7 us (1%)
  local copies, waits for them, and re-layouts  14.9 us (1%)
    psum x3, waiting for transfers between devices, spread(): return lax.psum(kept, axis)  807 us
    all_to_all x3, blocking collectives, across_cols(): lax.all_to_all(pieces, 'col', split_axis=1, concat_axis=1, tiled=True)  86.2 us
    all_to_all x2, blocking collectives, mirrored(): lax.all_to_all(by_target, 'row', split_axis=0, concat_axis=0, tiled=True)  47.8 us
    ppermute x4, waiting for transfers between devices, swapped(): return lax.ppermute(value, axis, pairs)  47.4 us
    all_to_all x5, waiting for transfers between devices, across_cols(): lax.all_to_all(pieces, 'col', split_axis=1, concat_axis=1, tiled=True)  44.9 us
    all_to_all x2, waiting for transfers between devices, mirrored(): lax.all_to_all(by_target, 'row', split_axis=0, concat_axis=0, tiled=True)  28 us
    all_to_all x5, starting transfers between devices, across_cols(): lax.all_to_all(pieces, 'col', split_axis=1, concat_axis=1, tiled=True)  25.6 us
  transfers between devices with their start and end apart: 16, of which 14 were waited for; matrix products, arithmetic and copies ran while one was open for 3% of the time, Pallas kernels for 0%

commit v1 on v0

--- a/solution.py
+++ b/solution.py
@@ -43,7 +43,10 @@
 
 
 def across_cols(pieces):
-    return lax.all_to_all(pieces, "col", split_axis=1, concat_axis=1, tiled=True)
+    return jnp.concatenate(
+        lax.all_to_all(jnp.stack(jnp.split(pieces, lax.axis_size("col"), axis=1)), "col", 0, 0),
+        axis=1,
+    )
 
 
 def mirrored(tile_set):

time: 1220 us -> 1250 us (1.025)
  local copies, waits for them, and re-layouts: 14.9 us -> 74.2 us
  blocking collectives: 134 us -> 100 us
  waiting for transfers between devices: 948 us -> 922 us
  starting transfers between devices: 77.8 us -> 103 us
    unnamed x12 -> x134, local copies, waits for them, and re-layouts: 0.24 us -> 58.6 us
    all_to_all x3 -> x2, blocking collectives: 86.2 us -> 53.3 us  [across_cols(): lax.all_to_all(jnp.stack(jnp.split(pieces, lax.axis_size('col'), axis=1))...]
    all_to_all x2, waiting for transfers between devices: 28 us -> 6.73 us  [mirrored(): lax.all_to_all(by_target, 'row', split_axis=0, concat_axis=0, tiled=True)]
    all_to_all x5 -> x6, starting transfers between devices: 25.6 us -> 43.1 us  [across_cols(): lax.all_to_all(jnp.stack(jnp.split(pieces, lax.axis_size('col'), axis=1))...]
    all_to_all x5 -> x6, waiting for transfers between devices: 44.9 us -> 46.1 us  [across_cols(): lax.all_to_all(jnp.stack(jnp.split(pieces, lax.axis_size('col'), axis=1))...]
  transfers between devices with their start and end apart: 16 -> 17, of which waited for: 14 -> 14; matrix products, arithmetic and copies ran while one was open for 3% -> 5% of each run, Pallas kernels for 0% -> 0%
where the time goes in v1:
time: 1250 us
  waiting for transfers between devices  922 us (74%)
  starting transfers between devices  103 us (8%)
  blocking collectives  100 us (8%)
  local copies, waits for them, and re-layouts  74.2 us (6%)
  matrix products  27.1 us (2%)
  between operations  18.1 us (1%)
    psum x3, waiting for transfers between devices, spread(): return lax.psum(kept, axis)  808 us
    unnamed x134, local copies, waits for them, and re-layouts  58.6 us
    all_to_all x2, blocking collectives, across_cols(): lax.all_to_all(jnp.stack(jnp.split(pieces, lax.axis_size('col'), axis=1))...  53.3 us
    all_to_all x2, blocking collectives, mirrored(): lax.all_to_all(by_target, 'row', split_axis=0, concat_axis=0, tiled=True)  47 us
    all_to_all x6, waiting for transfers between devices, across_cols(): lax.all_to_all(jnp.stack(jnp.split(pieces, lax.axis_size('col'), axis=1))...  46.1 us
    all_to_all x6, starting transfers between devices, across_cols(): lax.all_to_all(jnp.stack(jnp.split(pieces, lax.axis_size('col'), axis=1))...  43.1 us
    ppermute x4, waiting for transfers between devices, swapped(): return lax.ppermute(value, axis, pairs)  40.6 us
  transfers between devices with their start and end apart: 17, of which 14 were waited for; matrix products, arithmetic and copies ran while one was open for 5% of the time, Pallas kernels for 0%

profile of v1, /device:TPU:1, one launch (start us, length us, event | category | flops | bytes accessed | tf_op | source)
XLA Modules:
  0.0 1247.8 jit_solution(11327798257530110574)
XLA Ops:
  17.2 16.3 %all-to-all-start.3 = ((f32[16,2,1,16,256]{4,3,1,2,0:T(8,128)}), f32[16,2,1,16,256]{4,3,1,2,0:T(8,128)S(1)}, u32[]{:S(2)}, u32[]{:S(2)}) async-start(f32[16,2,1,16,256]{4,3,1,2,0:T(8,128)} %constant_dynamic-update-slice_fusion.32), calls=%async_computation.3 | async-start | bytes 1048576 | tf_op jit(solution)/shard_map/all_to_all | solution.py:47
  51.6 6.3 all-to-all-start
  58.8 16.2 %all-to-all-done = f32[16,2,1,16,256]{4,3,1,2,0:T(8,128)S(1)} async-done(((f32[16,2,1,16,256]{4,3,1,2,0:T(8,128)}), f32[16,2,1,16,256]{4,3,1,2,0:T(8,128)S(1)}, u32[]{:S(2)}, u32[]{:S(2)}) %all-to-all-start) | async-done | bytes 524320 | tf_op jit(solution)/shard_map/all_to_all | solution.py:47
  74.9 10.1 all-to-all-start.4
  89.4 11.3 collective-permute-done
  104.6 8.7 all-to-all-start.1
  123.0 6.7 all-to-all-done.1
  145.1 9.2 all-to-all-done.5
  160.3 7.1 collective-permute-start.2
  169.5 23.9 %collective-permute-done.2 = f32[2,256,256]{2,1,0:T(8,128)} collective-permute-done((f32[2,256,256]{2,1,0:T(8,128)}, f32[2,256,256]{2,1,0:T(8,128)}, u32[]{:S(2)}, u32[]{:S(2)}) %collective-permute-start.2) | collective-permute-done | bytes 524320 | tf_op jit(solution)/shard_map/ppermute | solution.py:15
  193.4 7.3 collective-permute-start.3
  221.5 271.6 %all-reduce.11.cloned.1.call-done = (f32[1,256,256]{2,1,0:T(8,128)}, f32[1,256,256]{2,1,0:T(8,128)}) async-done(((f32[1,256,256]{2,1,0:T(8,128)}, f32[1,256,256]{2,1,0:T(8,128)}), (f32[1,256,256]{2,1,0:T(8,128)}, f32[1,256,256]{2,1,0:T(8,128)})) %all-reduce.11.cloned.1.call-update) | async-done | bytes 524304 | tf_op jit(solution)/shard_map/psum | solution.py:26
  495.1 26.7 %all_to_all.60 = f32[16,2,1,16,256]{4,3,1,2,0:T(8,128)S(1)} all-to-all(f32[16,2,1,16,256]{4,3,1,2,0:T(8,128)S(1)} %constant_dynamic-update-slice_fusion.65), channel_id=1, replica_groups=mesh['row'=32,'col'=16] {'col'}, dimensions={0} | all-to-all | bytes 1048576 | tf_op jit(solution)/shard_map/all_to_all | solution.py:47
  521.8 23.5 %all_to_all.61 = f32[32,16,256]{2,1,0:T(8,128)S(1)} all-to-all(f32[32,16,256]{2,1,0:T(8,128)S(1)} %bitcast.1038), channel_id=1, replica_groups=mesh['row'=32,'col'=16] {'row'}, dimensions={0} | all-to-all | bytes 1048576 | tf_op jit(solution)/shard_map/all_to_all | solution.py:59
  561.4 9.5 collective-permute-start.4
  571.0 8.2 all-to-all-done.8
  585.7 9.1 collective-permute-done.4
  597.2 270.2 %all-reduce.9.cloned.1.call-done = (f32[1,256,256]{2,1,0:T(8,128)}, f32[1,256,256]{2,1,0:T(8,128)}) async-done(((f32[1,256,256]{2,1,0:T(8,128)}, f32[1,256,256]{2,1,0:T(8,128)}), (f32[1,256,256]{2,1,0:T(8,128)}, f32[1,256,256]{2,1,0:T(8,128)})) %all-reduce.9.cloned.1.call-update) | async-done | bytes 524304 | tf_op jit(solution)/shard_map/psum | solution.py:26
  869.5 26.7 %all_to_all.62 = f32[16,2,1,16,256]{4,3,1,2,0:T(8,128)S(1)} all-to-all(f32[16,2,1,16,256]{4,3,1,2,0:T(8,128)S(1)} %constant_dynamic-update-slice_fusion.97), channel_id=1, replica_groups=mesh['row'=32,'col'=16] {'col'}, dimensions={0} | all-to-all | bytes 1048576 | tf_op jit(solution)/shard_map/all_to_all | solution.py:47
  896.2 23.5 %all_to_all.63 = f32[32,16,256]{2,1,0:T(8,128)S(1)} all-to-all(f32[32,16,256]{2,1,0:T(8,128)S(1)} %bitcast.1039), channel_id=1, replica_groups=mesh['row'=32,'col'=16] {'row'}, dimensions={0} | all-to-all | bytes 1048576 | tf_op jit(solution)/shard_map/all_to_all | solution.py:59
  935.8 10.5 collective-permute-start.5
  946.2 7.3 all-to-all-done.11
  960.1 11.4 collective-permute-done.5
  972.1 266.6 %all-reduce.7.cloned.1.call-done = (f32[1,256,256]{2,1,0:T(8,128)}, f32[1,256,256]{2,1,0:T(8,128)}) async-done(((f32[1,256,256]{2,1,0:T(8,128)}, f32[1,256,256]{2,1,0:T(8,128)}), (f32[1,256,256]{2,1,0:T(8,128)}, f32[1,256,256]{2,1,0:T(8,128)})) %all-reduce.7.cloned.1.call-update) | async-done | bytes 524304 | tf_op jit(solution)/shard_map/psum | solution.py:26
  (244 shorter events, 142.0 us)
Async XLA Ops:
  6.5 32.5 %copy-start.4 = (f32[1,2,1,256,256]{4,3,2,1,0:T(8,128)S(1)}, f32[1,2,1,256,256]{4,3,2,1,0:T(8,128)}, u32[]{:S(2)}) copy-start(f32[1,2,1,256,256]{4,3,2,1,0:T(8,128)} %param.5) | copy-start | bytes 1572868
  17.2 67.9 %copy-start.6 = (f32[1,2,1,256,256]{4,3,2,1,0:T(8,128)S(1)}, f32[1,2,1,256,256]{4,3,2,1,0:T(8,128)}, u32[]{:S(2)}) copy-start(f32[1,2,1,256,256]{4,3,2,1,0:T(8,128)} %param.6) | copy-start | bytes 1572868
  17.2 71.4 %copy-start = (f32[1,256,256]{2,1,0:T(8,128)S(1)}, f32[1,256,256]{2,1,0:T(8,128)}, u32[]{:S(2)}) copy-start(f32[1,256,256]{2,1,0:T(8,128)} %param.7) | copy-start | bytes 786436
  17.2 34.4 %all-to-all-start.3 = ((f32[16,2,1,16,256]{4,3,1,2,0:T(8,128)}), f32[16,2,1,16,256]{4,3,1,2,0:T(8,128)S(1)}, u32[]{:S(2)}, u32[]{:S(2)}) async-start(f32[16,2,1,16,256]{4,3,1,2,0:T(8,128)} %constant_dynamic-update-slice_fusion.32), calls=%async_computation.3 | async-start | bytes 1048576 | tf_op jit(solution)/shard_map/all_to_all | solution.py:47
  51.6 23.3 %all-to-all-start = ((f32[16,2,1,16,256]{4,3,1,2,0:T(8,128)}), f32[16,2,1,16,256]{4,3,1,2,0:T(8,128)S(1)}, u32[]{:S(2)}, u32[]{:S(2)}) async-start(f32[16,2,1,16,256]{4,3,1,2,0:T(8,128)} %constant_dynamic-update-slice_fusion), calls=%async_computation | async-start | bytes 1048576 | tf_op jit(solution)/shard_map/all_to_all | solution.py:47
  74.9 29.7 %all-to-all-start.4 = ((f32[32,16,256]{2,1,0:T(8,128)}), f32[32,16,256]{2,1,0:T(8,128)S(1)}, u32[]{:S(2)}, u32[]{:S(2)}) async-start(f32[32,16,256]{2,1,0:T(8,128)} %bitcast.62), calls=%async_computation.4 | async-start | bytes 1048576 | tf_op jit(solution)/shard_map/all_to_all | solution.py:59
  85.1 15.6 %collective-permute-start = (f32[2,256,256]{2,1,0:T(8,128)S(1)}, f32[2,256,256]{2,1,0:T(8,128)}, u32[]{:S(2)}, u32[]{:S(2)}) collective-permute-start(f32[2,256,256]{2,1,0:T(8,128)S(1)} %bitcast.1043), channel_id=1, source_target_pairs={{0,1},{1,0},{2,3},{3,2},{4,5},{5,4},{6,7},{7,6},{8,9},{9,8},{10,11... | collective-permute-start | bytes 1572872 | tf_op jit(solution)/shard_map/ppermute | solution.py:15
  100.7 59.6 %collective-permute-start.1 = (f32[2,256,256]{2,1,0:T(8,128)}, f32[2,256,256]{2,1,0:T(8,128)}, u32[]{:S(2)}, u32[]{:S(2)}) collective-permute-start(f32[2,256,256]{2,1,0:T(8,128)} %collective-permute-done), channel_id=1, source_target_pairs={{0,2},{1,3},{2,0},{3,1},{4,6},{5,7},{6,4},{7,5},{8,10},{9,11},{10,... | collective-permute-start | bytes 1572872 | tf_op jit(solution)/shard_map/ppermute | solution.py:15
  104.6 25.1 %all-to-all-start.1 = ((f32[32,16,256]{2,1,0:T(8,128)}), f32[32,16,256]{2,1,0:T(8,128)S(1)}, u32[]{:S(2)}, u32[]{:S(2)}) async-start(f32[32,16,256]{2,1,0:T(8,128)} %bitcast.22), calls=%async_computation.1 | async-start | bytes 1048576 | tf_op jit(solution)/shard_map/all_to_all | solution.py:59
  129.7 24.6 %all-to-all-start.5 = ((f32[16,2,1,16,256]{4,3,1,2,0:T(8,128)}), f32[16,2,1,16,256]{4,3,1,2,0:T(8,128)S(1)}, u32[]{:S(2)}, u32[]{:S(2)}) async-start(f32[16,2,1,16,256]{4,3,1,2,0:T(8,128)} %constant_dynamic-update-slice_fusion.48), calls=%async_computation.5 | async-start | bytes 1048576 | tf_op jit(solution)/shard_map/all_to_all | solution.py:47
  154.3 47.3 %all-to-all-start.2 = ((f32[16,2,1,16,256]{4,3,1,2,0:T(8,128)}), f32[16,2,1,16,256]{4,3,1,2,0:T(8,128)}, u32[]{:S(2)}, u32[]{:S(2)}) async-start(f32[16,2,1,16,256]{4,3,1,2,0:T(8,128)} %constant_dynamic-update-slice_fusion.16), calls=%async_computation.2 | async-start | bytes 1048576 | tf_op jit(solution)/shard_map/all_to_all | solution.py:47
  159.6 333.4 %all-reduce.11.cloned.1.call-start = ((), (), s32[]{:S(2)}) async-start(), calls=%async_computation.14 | async-start | bytes 1048576 | tf_op jit(solution)/shard_map/psum | solution.py:26
  160.3 33.1 %collective-permute-start.2 = (f32[2,256,256]{2,1,0:T(8,128)}, f32[2,256,256]{2,1,0:T(8,128)}, u32[]{:S(2)}, u32[]{:S(2)}) collective-permute-start(f32[2,256,256]{2,1,0:T(8,128)} %collective-permute-done.1), channel_id=1, source_target_pairs={{0,4},{1,5},{2,6},{3,7},{4,0},{5,1},{6,2},{7,3},{8,12},{9,13},{10,... | collective-permute-start | bytes 1572872 | tf_op jit(solution)/shard_map/ppermute | solution.py:15
  193.4 25.7 %collective-permute-start.3 = (f32[2,256,256]{2,1,0:T(8,128)}, f32[2,256,256]{2,1,0:T(8,128)}, u32[]{:S(2)}, u32[]{:S(2)}) collective-permute-start(f32[2,256,256]{2,1,0:T(8,128)} %collective-permute-done.2), channel_id=1, source_target_pairs={{0,8},{1,9},{2,10},{3,11},{4,12},{5,13},{6,14},{7,15},{8,0},{9,1},... | collective-permute-start | bytes 1572872 | tf_op jit(solution)/shard_map/ppermute | solution.py:15
  201.6 3.6 copy-start.5
  209.0 3.3 copy-start.1
  555.2 24.0 %all-to-all-start.8 = ((f32[16,2,1,16,256]{4,3,1,2,0:T(8,128)}), f32[16,2,1,16,256]{4,3,1,2,0:T(8,128)S(1)}, u32[]{:S(2)}, u32[]{:S(2)}) async-start(f32[16,2,1,16,256]{4,3,1,2,0:T(8,128)} %constant_dynamic-update-slice_fusion.81), calls=%async_computation.8 | async-start | bytes 1048576 | tf_op jit(solution)/shard_map/all_to_all | solution.py:47
  560.1 307.3 %all-reduce.9.cloned.1.call-start = ((), (), s32[]{:S(2)}) async-start(), calls=%async_computation.13 | async-start | bytes 1048576 | tf_op jit(solution)/shard_map/psum | solution.py:26
  561.4 33.4 %collective-permute-start.4 = (f32[2,256,256]{2,1,0:T(8,128)}, f32[2,256,256]{2,1,0:T(8,128)}, u32[]{:S(2)}, u32[]{:S(2)}) collective-permute-start(f32[2,256,256]{2,1,0:T(8,128)} %collective-permute-done.3), channel_id=1, source_target_pairs={{1,0},{2,1},{3,2},{4,3},{5,4},{6,5},{7,6},{8,7},{9,8},{10,9},{11,1... | collective-permute-start | bytes 1572872 | tf_op jit(solution)/shard_map/ppermute | solution.py:21
  579.4 1.7 copy-start.2
  929.6 24.0 %all-to-all-start.11 = ((f32[16,2,1,16,256]{4,3,1,2,0:T(8,128)}), f32[16,2,1,16,256]{4,3,1,2,0:T(8,128)S(1)}, u32[]{:S(2)}, u32[]{:S(2)}) async-start(f32[16,2,1,16,256]{4,3,1,2,0:T(8,128)} %constant_dynamic-update-slice_fusion.113), calls=%async_computation.11 | async-start | bytes 1048576 | tf_op jit(solution)/shard_map/all_to_all | solution.py:47
  934.4 304.3 %all-reduce.7.cloned.1.call-start = ((), (), s32[]{:S(2)}) async-start(), calls=%async_computation.12 | async-start | bytes 1048576 | tf_op jit(solution)/shard_map/psum | solution.py:26
  935.8 35.7 %collective-permute-start.5 = (f32[2,256,256]{2,1,0:T(8,128)}, f32[2,256,256]{2,1,0:T(8,128)S(1)}, u32[]{:S(2)}, u32[]{:S(2)}) collective-permute-start(f32[2,256,256]{2,1,0:T(8,128)} %collective-permute-done.3), channel_id=1, source_target_pairs={{2,0},{3,1},{4,2},{5,3},{6,4},{7,5},{8,6},{9,7},{10,8},{11,9},{12,... | collective-permute-start | bytes 1572872 | tf_op jit(solution)/shard_map/ppermute | solution.py:21
  953.7 1.7 copy-start.3
Sparse Core Ops, SparseCore 0:
  213.7 279.3 all-reduce.10
  585.8 281.5 all-reduce.8
  960.2 278.5 all-reduce.6
